TPU v7x, 32 devices: a whole 2x2x4 slice. The times are simulated.
32 devices in a mesh: ens: 2 (over y), grid: 16 (over z, x, core).
Axes of the slice: x: 2, y: 2, z: 4, core: 2. Of those that a mesh axis runs over, the one named last changes fastest.
Arguments:
- fields: bfloat16 [2, 384, 768, 256], P('ens', 'grid'), may hold values from -6 to 6
- mode_counts: int32 [384], P('grid'), may hold values from 96 to 384, as said below
- gain_attn: float32 [256], replicated, may hold values from 0.5 to 1.5
- w_query: bfloat16 [256, 256], replicated, may hold values from -1 to 1
- w_key: bfloat16 [256, 256], replicated, may hold values from -8 to 8
- w_value: bfloat16 [256, 256], replicated, may hold values from -0.375 to 0.375
- w_out: bfloat16 [256, 256], replicated, may hold values from -0.375 to 0.375
- gain_spec: float32 [256], replicated, may hold values from 0.5 to 1.5
- w_first: bfloat16 [2, 8, 32, 32], replicated, may hold values from -1 to 1
- w_second: bfloat16 [2, 8, 32, 32], replicated, may hold values from -1 to 1
Outputs:
- layer_out: bfloat16 [2, 384, 768, 256], P('ens', 'grid')
Inputs may be any that keep to these rules, and one draw needn't show every extreme that they name: `mode_counts`: longitude wavenumbers kept in each latitude row; some row keeps all 384.
All inputs are finite; a program needn't handle non-finite values.
Results may differ from a plain program's by a relative error of at most 0.012.
Values may be sent and summed in bfloat16 or wider, within the bound.
A program may use at most 256 MiB of HBM per device.

v0:
```python
import functools
import math

import jax
import jax.numpy as jnp
import numpy as np
from jax import lax
from jax.experimental import pallas as pl
from jax.experimental.pallas import tpu as pltpu
from jax.sharding import PartitionSpec as P

HEAD = 32
NLAT = 384
KLON = 384
KLAT = 128
CHUNKS = 6
BACK_CHUNKS = 2

MESH = pl.DeviceIdType.MESH
SWAP_AHEAD = 6
ARRIVE_LAG = 3
PACK = 16

norm_eps = 1e-05


def layer_norm(widened, gain_vec):
    center = widened - jnp.mean(widened, axis=-1, keepdims=True)
    spread = jnp.mean(center * center, axis=-1, keepdims=True)
    return (center * lax.rsqrt(spread + norm_eps) * gain_vec).astype(jnp.bfloat16)


def wave_order(groups):
    held = KLON // groups
    place = jnp.arange(2 * KLON, dtype=jnp.int32)
    part = place // held % 2
    wave = place // (2 * held) * held + place % held
    return part, wave


def lon_forward(points, groups):
    part, wave = wave_order(groups)
    positions = jnp.arange(points, dtype=jnp.int32)
    turn_count = wave[:, None] * positions[None, :] % points
    angles = 2.0 * math.pi / points * turn_count.astype(jnp.float32)
    factor = 1.0 / math.sqrt(points)
    return jnp.where(
        part[:, None] == 0, jnp.cos(angles) * factor, -jnp.sin(angles) * factor
    ).astype(jnp.bfloat16)


def lon_inverse(points, groups):
    part, wave = wave_order(groups)
    positions = jnp.arange(points, dtype=jnp.int32)
    turn_count = positions[:, None] * wave[None, :] % points
    angles = 2.0 * math.pi / points * turn_count.astype(jnp.float32)
    weight = jnp.where(wave == 0, 1.0, 2.0).astype(jnp.float32)[None, :] / math.sqrt(points)
    return jnp.where(
        part[None, :] == 0, jnp.cos(angles) * weight, -jnp.sin(angles) * weight
    ).astype(jnp.bfloat16)


def lat_angles(row_count, mode_count):
    frequency = jnp.arange(mode_count, dtype=jnp.int32)
    frequency = jnp.where(frequency < mode_count // 2, frequency, frequency - mode_count)
    positions = jnp.arange(row_count, dtype=jnp.int32)
    turn_count = frequency[:, None] * positions[None, :] % row_count
    return 2.0 * math.pi / row_count * turn_count.astype(jnp.float32)


def lat_forward(row_count, mode_count):
    angles = lat_angles(row_count, mode_count)
    factor = 1.0 / math.sqrt(row_count)
    cosine = jnp.cos(angles) * factor
    sine_part = jnp.sin(angles) * factor
    return jnp.stack(
        [jnp.stack([cosine, sine_part], axis=1), jnp.stack([-sine_part, cosine], axis=1)]
    ).astype(jnp.bfloat16)


def lat_inverse(row_count, mode_count):
    angles = jnp.transpose(lat_angles(row_count, mode_count))
    factor = 1.0 / math.sqrt(row_count)
    cosine = jnp.cos(angles) * factor
    sine_part = jnp.sin(angles) * factor
    return jnp.stack([jnp.stack([cosine, -sine_part]), jnp.stack([sine_part, cosine])]).astype(
        jnp.bfloat16
    )


def complex_blocks(weight):
    real_part = weight[0]
    imag_part = weight[1]
    return jnp.stack([jnp.stack([real_part, imag_part]), jnp.stack([-imag_part, real_part])])


def mix_blocks(spec, big):
    blocks = spec.reshape(spec.shape[:3] + (big.shape[2], big.shape[3]))
    out_blocks = jnp.einsum("pqkbi,psbio->sqkbo", blocks, big, preferred_element_type=jnp.float32)
    return out_blocks.reshape(spec.shape)


def dot(left, right):
    return jnp.dot(left, right, preferred_element_type=jnp.float32)


def attend_kernel(others, first_row, sub, counts, own, *refs):
    other_refs = refs[:others]
    (gain_one, w_qkv, w_out, gain_two, table, sums, waves, attended, spectrum, normed) = refs[others:]
    points, feat = own.shape[1:]
    scale = 1.0 / math.sqrt(HEAD)
    for start in range(0, points, sub):
        rows = pl.ds(start, sub)
        fields = own[0, rows, :].astype(jnp.float32)
        joined = dot(layer_norm(fields, gain_one[...]), w_qkv[...]).astype(jnp.bfloat16)
        queries = joined[:, :feat].astype(jnp.float32)
        own_keys = joined[:, feat : 2 * feat].astype(jnp.float32)
        values = [joined[:, 2 * feat :].astype(jnp.float32)]
        shifted = [jnp.zeros((sub, feat), jnp.float32)]
        for ref in other_refs:
            side = layer_norm(ref[0, rows, :].astype(jnp.float32), gain_one[...])
            pair = dot(side, w_qkv[:, feat:]).astype(jnp.bfloat16)
            terms = queries * (pair[:, :feat].astype(jnp.float32) - own_keys)
            upper = terms.astype(jnp.bfloat16)
            lower = (terms - upper.astype(jnp.float32)).astype(jnp.bfloat16)
            total = dot(upper, sums[...]) + dot(lower, sums[...])
            shifted.append(total * scale)
            values.append(pair[:, feat:].astype(jnp.float32))
        largest = functools.reduce(jnp.maximum, shifted)
        exps = [jnp.exp(item - largest) for item in shifted]
        totals = functools.reduce(jnp.add, exps)
        mixed = functools.reduce(
            jnp.add,
            [e.astype(jnp.bfloat16).astype(jnp.float32) * v for e, v in zip(exps, values)],
        )
        mixed = (mixed / totals).astype(jnp.bfloat16)
        result = (fields + dot(mixed, w_out[...])).astype(jnp.bfloat16)
        attended[0, rows, :] = result
        normed[rows, :] = layer_norm(result.astype(jnp.float32), gain_two[...])
    kept = waves[...] < counts[first_row + pl.program_id(0)]
    spec = dot(table[...], normed[...])
    spec = jnp.where(kept, spec, 0.0).astype(jnp.bfloat16)
    if len(spectrum.shape) == 4:
        spectrum[:, 0] = spec.reshape(spectrum.shape[0], spectrum.shape[2], feat)
    else:
        spectrum[0] = spec


def attend(chunk, rows, aligned, groups, fields, others, counts, gains, weights, tables):
    points, feat = fields.shape[1:]
    first_row = chunk * rows
    sub = points // 3 if points % 48 == 0 else points
    whole = lambda a: pl.BlockSpec(a.shape, lambda i, c: (0,) * a.ndim)
    w_qkv, w_out = weights
    table, sums, waves = tables
    held = 2 * KLON // groups
    if aligned:
        spec_shape = (groups, rows, held, feat)
        spec_block = pl.BlockSpec((groups, 1, held, feat), lambda i, c: (0, i, 0, 0))
    else:
        spec_shape = (rows, 2 * KLON, feat)
        spec_block = pl.BlockSpec((1, 2 * KLON, feat), lambda i, c: (i, 0, 0))
    row_block = pl.BlockSpec((1, points, feat), lambda i, c: (i, 0, 0))
    own_block = pl.BlockSpec((1, points, feat), lambda i, c: (first_row + i, 0, 0))
    params = (gains[0], w_qkv, w_out, gains[1], table, sums, waves)
    flops = 2 * rows * points * feat * (feat * 8 + 2 * KLON)
    attended, spectrum = pl.pallas_call(
        functools.partial(attend_kernel, len(others), first_row, sub),
        grid_spec=pltpu.PrefetchScalarGridSpec(
            num_scalar_prefetch=1,
            grid=(rows,),
            in_specs=[own_block] + [row_block] * len(others) + [whole(p) for p in params],
            out_specs=[row_block, spec_block],
            scratch_shapes=[pltpu.VMEM((points, feat), jnp.bfloat16)],
        ),
        out_shape=[
            jax.ShapeDtypeStruct((rows, points, feat), jnp.bfloat16),
            jax.ShapeDtypeStruct(spec_shape, jnp.bfloat16),
        ],
        cost_estimate=pl.CostEstimate(
            flops=flops, bytes_accessed=rows * points * feat * 8, transcendentals=rows * points * feat * 2
        ),
        compiler_params=pltpu.CompilerParams(vmem_limit_bytes=40 * 1024 * 1024),
    )(counts, fields, *others, *params)
    if not aligned:
        spectrum = jnp.transpose(spectrum.reshape(rows, groups, held, feat), (1, 0, 2, 3))
    return attended, spectrum


def finish_kernel(first_row, counts, spectrum, attended, table, waves, *refs):
    out = refs[-1]
    feat = out.shape[-1]
    kept = waves[...] < counts[first_row + pl.program_id(0)]
    if len(spectrum.shape) == 4:
        spec = spectrum[:, 0].reshape(2 * KLON, feat)
    else:
        spec = spectrum[0]
    spec = jnp.where(kept, spec.astype(jnp.float32), 0.0).astype(jnp.bfloat16)
    out[0] = (attended[0].astype(jnp.float32) + dot(table[...], spec)).astype(jnp.bfloat16)


def finish(first_row, offset, lat_dev, aligned, groups, spectrum, attended, counts, table, waves, so_far):
    rows, points, feat = attended.shape
    held = 2 * KLON // groups
    whole = lambda a: pl.BlockSpec(a.shape, lambda i, c: (0,) * a.ndim)
    if aligned:
        spec_block = pl.BlockSpec((groups, 1, held, feat), lambda i, c: (0, offset + i, 0, 0))
    else:
        spectrum = jnp.transpose(spectrum, (1, 0, 2, 3)).reshape(-1, 2 * KLON, feat)
        spec_block = pl.BlockSpec((1, 2 * KLON, feat), lambda i, c: (offset + i, 0, 0))
    row_block = pl.BlockSpec((1, points, feat), lambda i, c: (i, 0, 0))
    out_block = pl.BlockSpec((1, points, feat), lambda i, c: (first_row + i, 0, 0))
    operands = [counts, spectrum, attended, table, waves]
    specs = [spec_block, row_block, whole(table), whole(waves)]
    aliases = {}
    if so_far is not None:
        aliases = {len(operands): 0}
        operands.append(so_far)
        specs.append(pl.BlockSpec(memory_space=pl.ANY))
    return pl.pallas_call(
        functools.partial(finish_kernel, first_row),
        grid_spec=pltpu.PrefetchScalarGridSpec(
            num_scalar_prefetch=1, grid=(rows,), in_specs=specs, out_specs=out_block
        ),
        out_shape=jax.ShapeDtypeStruct((lat_dev, points, feat), jnp.bfloat16),
        input_output_aliases=aliases,
        cost_estimate=pl.CostEstimate(
            flops=4 * rows * points * feat * KLON,
            bytes_accessed=rows * points * feat * 6,
            transcendentals=0,
        ),
        compiler_params=pltpu.CompilerParams(vmem_limit_bytes=40 * 1024 * 1024),
    )(*operands)


def shards(
    mesh_sizes, fields, mode_counts, gain_attn, w_query, w_key, w_value, w_out, gain_spec, w_first, w_second
):
    members, groups = mesh_sizes
    fields = fields[0]
    lat_dev, points, feat = fields.shape
    held = KLON // groups
    aligned = (2 * held) % 16 == 0
    chunks = max(c for c in range(1, CHUNKS + 1) if lat_dev % c == 0)
    rows = lat_dev // chunks
    shifts = [
        [(i, (i + s) % members) for i in range(members)] for s in range(1, members)
    ]
    others = []
    for c in range(chunks):
        others.append([lax.ppermute(fields[c * rows : (c + 1) * rows], "ens", s) for s in shifts])
    w_qkv = jnp.concatenate([w_query, w_key, w_value], axis=1)
    lanes = jnp.arange(feat, dtype=jnp.int32) // HEAD
    sums = (lanes[:, None] == lanes[None, :]).astype(jnp.bfloat16)
    waves = wave_order(groups)[1][:, None]
    gains = (gain_attn[None, :], gain_spec[None, :])
    tables = (lon_forward(points, groups), sums, waves)
    back_table = lon_inverse(points, groups)
    forward = lat_forward(NLAT, KLAT).reshape(2, KLAT, 2, groups, chunks, rows)
    backs = max(c for c in range(1, BACK_CHUNKS + 1) if chunks % c == 0)
    per_back = chunks // backs
    inverse = lat_inverse(NLAT, KLAT).reshape(2, 2, groups, backs, per_back * rows, KLAT)
    big_one = complex_blocks(w_first)
    big_two = complex_blocks(w_second)
    kept_fields = []
    rows_spec = None
    for c in range(chunks):
        attended, spectrum = attend(
            c, rows, aligned, groups, fields, others[c], mode_counts, gains, (w_qkv, w_out), tables
        )
        kept_fields.append(attended)
        arrived = lax.all_to_all(spectrum, "grid", split_axis=0, concat_axis=0)
        arrived = arrived.reshape(groups, rows, 2, held, feat)
        term = jnp.einsum(
            "pqrgj,gjrkd->pqkd",
            forward[:, :, :, :, c],
            arrived,
            preferred_element_type=jnp.float32,
        )
        rows_spec = term if rows_spec is None else rows_spec + term
        if c < chunks - 1:
            rows_spec = lax.optimization_barrier(rows_spec)
    rows_spec = rows_spec.astype(jnp.bfloat16)
    hidden = jnp.maximum(mix_blocks(rows_spec, big_one), 0.0).astype(jnp.bfloat16)
    second = mix_blocks(hidden, big_two).astype(jnp.bfloat16)
    out = None
    for b in range(backs):
        back_rows = jnp.einsum(
            "rpgjq,pqkd->gjrkd", inverse[:, :, :, b], second, preferred_element_type=jnp.float32
        ).astype(jnp.bfloat16)
        returned = lax.all_to_all(
            back_rows.reshape(groups, per_back * rows, 2 * held, feat), "grid", split_axis=0, concat_axis=0
        )
        for i in range(per_back):
            c = b * per_back + i
            out = finish(
                c * rows, i * rows, lat_dev, aligned, groups, returned, kept_fields[c], mode_counts,
                back_table, tables[2], out,
            )
    return out[None]


def np_wave_order(groups):
    held = KLON // groups
    place = np.arange(2 * KLON)
    return place // held % 2, place // (2 * held) * held + place % held


def np_lon_forward(points, groups):
    part, wave = np_wave_order(groups)
    turns = wave[:, None] * np.arange(points)[None, :] % points
    angles = 2.0 * math.pi / points * turns
    rows = np.where(part[:, None] == 0, np.cos(angles), -np.sin(angles)) / math.sqrt(points)
    return jnp.asarray(rows.astype(np.float32), dtype=jnp.bfloat16)


def np_lat_tables(groups, batches, nb):
    frequency = np.arange(KLAT)
    frequency = np.where(frequency < KLAT // 2, frequency, frequency - KLAT)
    angles = 2.0 * math.pi / NLAT * (frequency[:, None] * np.arange(NLAT)[None, :] % NLAT)
    cosine = np.cos(angles) / math.sqrt(NLAT)
    sine = np.sin(angles) / math.sqrt(NLAT)
    both = np.stack([np.stack([cosine, sine], axis=1), np.stack([-sine, cosine], axis=1)])
    forward = both.reshape(2, KLAT, 2, groups, batches, nb).transpose(4, 0, 1, 2, 5, 3)
    forward = forward.reshape(batches, 2 * KLAT, 2 * nb * groups).astype(np.float32)
    inverse = forward.transpose(0, 2, 1)
    return jnp.asarray(forward, dtype=jnp.bfloat16), jnp.asarray(inverse, dtype=jnp.bfloat16)


def np_turn(groups):
    count = groups * PACK
    source = np.arange(count).reshape(groups, PACK).T.reshape(-1)
    turn = np.zeros((count, count), np.float32)
    turn[np.arange(count), source] = 1.0
    return jnp.asarray(turn, dtype=jnp.bfloat16)


def layer_kernel(
    points_sub,
    nb,
    counts,
    fields,
    gain_one,
    w_query,
    w_key,
    w_value,
    w_out,
    gain_two,
    table,
    sums,
    waves,
    forward,
    inverse,
    turn,
    turn_back,
    spread,
    w_first,
    w_second,
    out,
    own,
    other,
    attended,
    sent,
    arrived,
    turned,
    rows_spec,
    second,
    normed,
    back_table,
    blocks,
    result,
    own_sem,
    swap_send,
    swap_recv,
    fwd_send,
    fwd_recv,
    back_send,
    back_recv,
    out_sem,
):
    rows, groups, width, feat = sent.shape
    points = other.shape[1]
    held = width // 2
    packs = width // PACK
    sub = points_sub
    member = lax.axis_index("ens")
    me = lax.axis_index("grid")
    scale = 1.0 / math.sqrt(HEAD)
    partners = [me ^ o for o in range(groups - 1, 0, -1)]

    barrier = pltpu.get_barrier_semaphore()
    for t in partners:
        pl.semaphore_signal(barrier, inc=1, device_id={"grid": t}, device_id_type=MESH)
    pl.semaphore_signal(barrier, inc=1, device_id={"ens": 1 - member}, device_id_type=MESH)
    pl.semaphore_wait(barrier, groups)

    def swap(r):
        return pltpu.make_async_remote_copy(
            src_ref=fields.at[r],
            dst_ref=other.at[r],
            send_sem=swap_send.at[r],
            recv_sem=swap_recv.at[r],
            device_id={"ens": 1 - member},
            device_id_type=MESH,
        )

    def fetch(r, slot):
        return pltpu.make_async_copy(fields.at[r], own.at[slot], own_sem.at[slot])

    ahead = min(SWAP_AHEAD, rows)
    for r in range(ahead):
        swap(r).start()
    fetch(0, 0).start()

    eye = lax.broadcasted_iota(jnp.int32, (feat, feat), 0) // HEAD
    same = eye == lax.broadcasted_iota(jnp.int32, (feat, feat), 1) // HEAD
    for layer, weight in enumerate((w_first, w_second)):
        for part in range(2):
            wide = dot(weight[part], spread[...])
            blocks[2 * layer + part] = jnp.where(same, wide, 0.0).astype(jnp.bfloat16)
    back_table[...] = jnp.transpose(table[...])
    rows_spec[...] = jnp.zeros_like(rows_spec)
    spot = pl.ds(pl.multiple_of(me * width, PACK), width)

    def attend(r):
        slot = lax.rem(r, 2)
        fetch(r, slot).wait()

        @pl.when(r + 1 < rows)
        def _():
            fetch(r + 1, 1 - slot).start()

        swap(r).wait_recv()

        @pl.when(r + ahead < rows)
        def _():
            swap(r + ahead).start()

        for start in range(0, points, sub):
            span = pl.ds(start, sub)
            field = own[slot, span, :].astype(jnp.float32)
            norm = layer_norm(field, gain_one[...])
            queries = dot(norm, w_query[...]).astype(jnp.bfloat16).astype(jnp.float32)
            own_keys = dot(norm, w_key[...]).astype(jnp.bfloat16).astype(jnp.float32)
            own_values = dot(norm, w_value[...]).astype(jnp.bfloat16).astype(jnp.float32)
            side = layer_norm(other[r, span, :].astype(jnp.float32), gain_one[...])
            keys = dot(side, w_key[...]).astype(jnp.bfloat16).astype(jnp.float32)
            values = dot(side, w_value[...]).astype(jnp.bfloat16).astype(jnp.float32)
            terms = queries * (keys - own_keys)
            upper = terms.astype(jnp.bfloat16)
            lower = (terms - upper.astype(jnp.float32)).astype(jnp.bfloat16)
            shifted = (dot(upper, sums[...]) + dot(lower, sums[...])) * scale
            largest = jnp.maximum(shifted, 0.0)
            own_exp = jnp.exp(-largest)
            side_exp = jnp.exp(shifted - largest)
            mixed = own_exp.astype(jnp.bfloat16).astype(jnp.float32) * own_values
            mixed += side_exp.astype(jnp.bfloat16).astype(jnp.float32) * values
            mixed = (mixed / (own_exp + side_exp)).astype(jnp.bfloat16)
            done = (field + dot(mixed, w_out[...])).astype(jnp.bfloat16)
            attended[r, span, :] = done
            normed[span, :] = layer_norm(done.astype(jnp.float32), gain_two[...])
        spec = dot(table[...], normed[...])
        spec = jnp.where(waves[...] < counts[r], spec, 0.0).astype(jnp.bfloat16)
        sent[r] = spec.reshape(groups, width, feat)
        arrived[r, me] = sent[r, me]
        for t in partners:
            pltpu.make_async_remote_copy(
                src_ref=sent.at[r, t],
                dst_ref=arrived.at[r, me],
                send_sem=fwd_send.at[r],
                recv_sem=fwd_recv.at[r],
                device_id={"grid": t},
                device_id_type=MESH,
            ).start()

    def turn_in(r):
        whole = arrived.at[r, pl.ds(0, groups - 1)]
        pltpu.make_async_copy(whole, whole, fwd_recv.at[r]).wait()
        place = pl.ds(pl.multiple_of(lax.rem(r, nb) * groups, PACK), groups)
        for b in range(packs):
            block = arrived[r, :, b * PACK : (b + 1) * PACK, :].reshape(groups * PACK, feat)
            moved = dot(turn[...], block).astype(jnp.bfloat16)
            turned[b * PACK : (b + 1) * PACK, place, :] = moved.reshape(PACK, groups, feat)

    def lat_in(b):
        def step(k, _):
            pair = jnp.concatenate([turned[k], turned[held + k]], axis=0)
            rows_spec[k] += dot(forward[b], pair)
            return 0

        lax.fori_loop(0, held, step, 0, unroll=4)

    def phase_in(i, _):
        @pl.when(i < rows)
        def _():
            attend(i)

        @pl.when(i >= ARRIVE_LAG)
        def _():
            turn_in(i - ARRIVE_LAG)

        @pl.when((i >= ARRIVE_LAG) & (lax.rem(i - ARRIVE_LAG, nb) == nb - 1))
        def _():
            lat_in((i - ARRIVE_LAG) // nb)

        return 0

    lax.fori_loop(0, rows + ARRIVE_LAG, phase_in, 0)

    half = second.shape[1] // 2
    per = max(p for p in range(1, 5) if held % p == 0)

    def complex_mix(real, imag, layer):
        w_real, w_imag = blocks[2 * layer], blocks[2 * layer + 1]
        return dot(real, w_real) - dot(imag, w_imag), dot(real, w_imag) + dot(imag, w_real)

    def mix(i, _):
        span = pl.ds(i * per, per)
        real = rows_spec[span, :half].reshape(per * half, feat).astype(jnp.bfloat16)
        imag = rows_spec[span, half:].reshape(per * half, feat).astype(jnp.bfloat16)
        real, imag = complex_mix(real, imag, 0)
        real = jnp.maximum(real, 0.0).astype(jnp.bfloat16)
        imag = jnp.maximum(imag, 0.0).astype(jnp.bfloat16)
        real, imag = complex_mix(real, imag, 1)
        second[span, :half] = real.astype(jnp.bfloat16).reshape(per, half, feat)
        second[span, half:] = imag.astype(jnp.bfloat16).reshape(per, half, feat)
        return 0

    lax.fori_loop(0, held // per, mix, 0)

    def wait_sent(r):
        whole = sent.at[r, pl.ds(0, groups - 1)]
        pltpu.make_async_copy(whole, whole, fwd_send.at[r]).wait()

    def lat_out(b):
        def step(k, _):
            both = dot(inverse[b], second[k]).astype(jnp.bfloat16)
            turned[k] = both[: nb * groups]
            turned[held + k] = both[nb * groups :]
            return 0

        lax.fori_loop(0, held, step, 0, unroll=4)

        def send_row(r, _):
            j = b * nb + r
            wait_sent(j)
            place = pl.ds(pl.multiple_of(r * groups, PACK), groups)
            for p in range(packs):
                block = turned[p * PACK : (p + 1) * PACK, place, :].reshape(groups * PACK, feat)
                moved = dot(turn_back[...], block).astype(jnp.bfloat16)
                sent[j, :, p * PACK : (p + 1) * PACK, :] = moved.reshape(groups, PACK, feat)
            other[j, spot, :] = sent[j, me]
            for t in partners:
                pltpu.make_async_remote_copy(
                    src_ref=sent.at[j, t],
                    dst_ref=other.at[j, spot],
                    send_sem=back_send.at[j],
                    recv_sem=back_recv.at[j],
                    device_id={"grid": t},
                    device_id_type=MESH,
                ).start()
            return 0

        lax.fori_loop(0, nb, send_row, 0)

    def put(j, slot):
        return pltpu.make_async_copy(result.at[slot], out.at[j], out_sem.at[slot])

    def finish(j):
        whole = other.at[j, pl.ds(0, (groups - 1) * width)]
        pltpu.make_async_copy(whole, whole, back_recv.at[j]).wait()
        weight = jnp.where(waves[...] == 0, 1.0, 2.0)
        weight = jnp.where(waves[...] < counts[j], weight, 0.0)
        spec = (other[j].astype(jnp.float32) * weight).astype(jnp.bfloat16)
        total = attended[j].astype(jnp.float32) + dot(back_table[...], spec)
        slot = lax.rem(j, 2)

        @pl.when(j >= 2)
        def _():
            put(j - 2, slot).wait()

        result[slot] = total.astype(jnp.bfloat16)
        put(j, slot).start()

    def phase_out(i, _):
        @pl.when((i < rows) & (lax.rem(i, nb) == 0))
        def _():
            lat_out(i // nb)

        @pl.when(i >= nb)
        def _():
            finish(i - nb)

        return 0

    lax.fori_loop(0, rows + nb, phase_out, 0)

    def drain(r, _):
        swap(r).wait_send()
        whole = sent.at[r, pl.ds(0, groups - 1)]
        pltpu.make_async_copy(whole, whole, back_send.at[r]).wait()
        return 0

    lax.fori_loop(0, rows, drain, 0)
    for j in range(rows - 2, rows):
        put(j, j % 2).wait()


def fused(mesh_sizes, fields, mode_counts, gain_attn, w_query, w_key, w_value, w_out, gain_spec, w_first, w_second):
    _, groups = mesh_sizes
    fields = fields[0]
    rows, points, feat = fields.shape
    width = 2 * KLON // groups
    held = width // 2
    nb = max(n for n in range(1, rows + 1) if rows % n == 0 and 2 * n * groups <= max(feat, 2 * groups))
    forward, inverse = np_lat_tables(groups, rows // nb, nb)
    turn = np_turn(groups)
    block = w_first.shape[-1]
    lanes = np.arange(feat)
    heads = jnp.asarray((lanes[:, None] // HEAD == lanes[None, :] // HEAD).astype(np.float32), dtype=jnp.bfloat16)
    spread = jnp.asarray((np.arange(block)[:, None] == lanes[None, :] % block).astype(np.float32), dtype=jnp.bfloat16)
    waves = jnp.asarray(np_wave_order(groups)[1][:, None], dtype=jnp.int32)
    operands = [
        mode_counts, fields, gain_attn[None, :], w_query, w_key, w_value, w_out, gain_spec[None, :],
        np_lon_forward(points, groups), heads, waves, forward, inverse, turn, turn.T, spread,
        w_first.reshape(2, feat, block), w_second.reshape(2, feat, block),
    ]
    vmem = pl.BlockSpec(memory_space=pltpu.VMEM)
    hbm = pl.BlockSpec(memory_space=pl.ANY)
    specs = [pl.BlockSpec(memory_space=pltpu.SMEM), hbm] + [vmem] * (len(operands) - 2)
    half = jnp.bfloat16
    dma = pltpu.SemaphoreType.DMA
    out = pl.pallas_call(
        functools.partial(layer_kernel, points // 3 if points % 48 == 0 else points, nb),
        in_specs=specs,
        out_specs=hbm,
        out_shape=jax.ShapeDtypeStruct((rows, points, feat), half),
        scratch_shapes=[
            pltpu.VMEM((2, points, feat), half),
            pltpu.VMEM((rows, points, feat), half),
            pltpu.VMEM((rows, points, feat), half),
            pltpu.VMEM((rows, groups, width, feat), half),
            pltpu.VMEM((rows, groups, width, feat), half),
            pltpu.VMEM((width, nb * groups, feat), half),
            pltpu.VMEM((held, 2 * KLAT, feat), jnp.float32),
            pltpu.VMEM((held, 2 * KLAT, feat), half),
            pltpu.VMEM((points, feat), half),
            pltpu.VMEM((points, 2 * KLON), half),
            pltpu.VMEM((4, feat, feat), half),
            pltpu.VMEM((2, points, feat), half),
            dma((2,)),
            dma((rows,)),
            dma((rows,)),
            dma((rows,)),
            dma((rows,)),
            dma((rows,)),
            dma((rows,)),
            dma((2,)),
        ],
        compiler_params=pltpu.CompilerParams(
            collective_id=0, has_side_effects=True, vmem_limit_bytes=67043328
        ),
        name="layer",
    )(*operands)
    return out[None]


def streams(members, groups, lat_dev, points, feat):
    width = 2 * KLON // groups
    return (
        members == 2
        and groups == PACK
        and (2 * KLON) % (groups * PACK) == 0
        and points == 2 * KLON
        and feat % 128 == 0
        and lat_dev % 2 == 0
        and width % PACK == 0
    )


def layer(mesh_sizes, *args):
    if streams(*mesh_sizes, *args[0].shape[1:]):
        return fused(mesh_sizes, *args)
    return shards(mesh_sizes, *args)


def solution(mesh):
    in_specs = (P("ens", "grid", None, None), P("grid"), P(), P(), P(), P(), P(), P(), P(), P())
    out_specs = P("ens", "grid", None, None)
    sizes = (mesh.shape["ens"], mesh.shape["grid"])
    return jax.shard_map(
        functools.partial(layer, sizes),
        mesh=mesh,
        in_specs=in_specs,
        out_specs=out_specs,
        check_vma=False,
    )
```

profile of v0, /device:TPU:0, one launch (start us, length us, event | category | flops | bytes accessed | tf_op | source)
XLA Modules:
  0.0 447.2 jit_solution(7825485439267830412)
XLA Ops:
  0.0 438.8 %layer.1 = bf16[24,768,256]{2,1,0:T(8,128)(2,1)} custom-call(s32[24]{0:T(128)} %counts.1, bf16[24,768,256]{2,1,0:T(8,128)(2,1)} %bitcast.7, f32[1,256]{1,0:T(1,128)} %bitcast.10, bf16[256,256]{1,0:T(8,128)(2,1)} %w_query.1, bf16[256,256]{1,0:T(8,128)(2,1)} %w_key.1, bf16[256,256]{1,0:T(8,128)(2,1)} %w_value.1, bf16[256,256]{1,0:T(8,128)(2,1)} %w_out.1, ...), custom_call_target="tpu_custom_call" | custom-call | tf_op jit(solution)/shard_map/layer/pallas_call | solution.py:633
  438.8 8.3 %copy.19 = bf16[1,24,768,256]{3,2,1,0:T(8,128)(2,1)} copy(bf16[1,24,768,256]{3,2,1,0:T(8,128)(2,1)} %bitcast.6) | data formatting | bytes 18874368
where the time goes:
time: 447 us
  Pallas kernels  439 us (98%)
  local copies, waits for them, and re-layouts  8.33 us (2%)
    pallas_call x1, Pallas kernels, fused(): pl.pallas_call(functools.partial(layer_kernel, points // 3 if points % 48...  439 us

commit v1 on v0

--- a/solution.py
+++ b/solution.py
@@ -302,8 +302,10 @@
 
 def np_wave_order(groups):
     held = KLON // groups
+    each = PACK // 2
     place = np.arange(2 * KLON)
-    return place // held % 2, place // (2 * held) * held + place % held
+    group, pack, within = place // (2 * held), place % (2 * held) // PACK, place % each
+    return place // each % 2, group * held + pack * each + within
 
 
 def np_lon_forward(points, groups):
@@ -323,7 +325,8 @@
     both = np.stack([np.stack([cosine, sine], axis=1), np.stack([-sine, cosine], axis=1)])
     forward = both.reshape(2, KLAT, 2, groups, batches, nb).transpose(4, 0, 1, 2, 5, 3)
     forward = forward.reshape(batches, 2 * KLAT, 2 * nb * groups).astype(np.float32)
-    inverse = forward.transpose(0, 2, 1)
+    inverse = both.reshape(2, KLAT, 2, 2, groups // 2, batches * nb).transpose(3, 2, 5, 4, 0, 1)
+    inverse = inverse.reshape(2, batches * nb * groups, 2 * KLAT).astype(np.float32)
     return jnp.asarray(forward, dtype=jnp.bfloat16), jnp.asarray(inverse, dtype=jnp.bfloat16)
 
 
@@ -352,7 +355,6 @@
     forward,
     inverse,
     turn,
-    turn_back,
     spread,
     w_first,
     w_second,
@@ -365,6 +367,7 @@
     turned,
     rows_spec,
     second,
+    far,
     normed,
     back_table,
     blocks,
@@ -374,6 +377,8 @@
     swap_recv,
     fwd_send,
     fwd_recv,
+    far_send,
+    far_recv,
     back_send,
     back_recv,
     out_sem,
@@ -382,11 +387,23 @@
     points = other.shape[1]
     held = width // 2
     packs = width // PACK
+    batches = rows // nb
     sub = points_sub
     member = lax.axis_index("ens")
     me = lax.axis_index("grid")
     scale = 1.0 / math.sqrt(HEAD)
     partners = [me ^ o for o in range(groups - 1, 0, -1)]
+    each = PACK // 2
+    half = groups // 2
+    quarter = groups // 4
+    side_at = me // half
+    far_side = 1 - side_at
+    place_at = lax.rem(me, half)
+    lane_at = lax.rem(me, quarter)
+    inner = me // quarter == 1 + side_at
+    relay = (1 + far_side) * quarter + lane_at
+    slot_at = jnp.where(inner, 0, 1)
+    relayed = packs - 1
 
     barrier = pltpu.get_barrier_semaphore()
     for t in partners:
@@ -420,7 +437,6 @@
             blocks[2 * layer + part] = jnp.where(same, wide, 0.0).astype(jnp.bfloat16)
     back_table[...] = jnp.transpose(table[...])
     rows_spec[...] = jnp.zeros_like(rows_spec)
-    spot = pl.ds(pl.multiple_of(me * width, PACK), width)
 
     def attend(r):
         slot = lax.rem(r, 2)
@@ -482,13 +498,15 @@
             moved = dot(turn[...], block).astype(jnp.bfloat16)
             turned[b * PACK : (b + 1) * PACK, place, :] = moved.reshape(PACK, groups, feat)
 
-    def lat_in(b):
-        def step(k, _):
-            pair = jnp.concatenate([turned[k], turned[held + k]], axis=0)
+    def lat_in(b, first, count):
+        def step(i, _):
+            k = first + i
+            at = k // each * PACK + lax.rem(k, each)
+            pair = jnp.concatenate([turned[at], turned[at + each]], axis=0)
             rows_spec[k] += dot(forward[b], pair)
             return 0
 
-        lax.fori_loop(0, held, step, 0, unroll=4)
+        lax.fori_loop(0, count, step, 0, unroll=4)
 
     def phase_in(i, _):
         @pl.when(i < rows)
@@ -499,111 +517,179 @@
         def _():
             turn_in(i - ARRIVE_LAG)
 
-        @pl.when((i >= ARRIVE_LAG) & (lax.rem(i - ARRIVE_LAG, nb) == nb - 1))
-        def _():
-            lat_in((i - ARRIVE_LAG) // nb)
+        b = (i - ARRIVE_LAG) // nb
+
+        @pl.when((i >= ARRIVE_LAG) & (lax.rem(i - ARRIVE_LAG, nb) == nb - 1) & (b < batches - 1))
+        def _():
+            lat_in(b, 0, held)
 
         return 0
 
     lax.fori_loop(0, rows + ARRIVE_LAG, phase_in, 0)
 
-    half = second.shape[1] // 2
-    per = max(p for p in range(1, 5) if held % p == 0)
+    mode = second.shape[1] // 2
 
     def complex_mix(real, imag, layer):
         w_real, w_imag = blocks[2 * layer], blocks[2 * layer + 1]
         return dot(real, w_real) - dot(imag, w_imag), dot(real, w_imag) + dot(imag, w_real)
 
-    def mix(i, _):
-        span = pl.ds(i * per, per)
-        real = rows_spec[span, :half].reshape(per * half, feat).astype(jnp.bfloat16)
-        imag = rows_spec[span, half:].reshape(per * half, feat).astype(jnp.bfloat16)
+    def ship(p):
+        span = pl.ds(p * each, each)
+        return pltpu.make_async_remote_copy(
+            src_ref=second.at[span],
+            dst_ref=far.at[slot_at, span],
+            send_sem=far_send.at[p],
+            recv_sem=far_recv.at[slot_at * relayed + p],
+            device_id={"grid": relay},
+            device_id_type=MESH,
+        )
+
+    def mix(p, _):
+        lat_in(batches - 1, p * each, each)
+        span = pl.ds(p * each, each)
+        real = rows_spec[span, :mode].reshape(each * mode, feat).astype(jnp.bfloat16)
+        imag = rows_spec[span, mode:].reshape(each * mode, feat).astype(jnp.bfloat16)
         real, imag = complex_mix(real, imag, 0)
         real = jnp.maximum(real, 0.0).astype(jnp.bfloat16)
         imag = jnp.maximum(imag, 0.0).astype(jnp.bfloat16)
         real, imag = complex_mix(real, imag, 1)
-        second[span, :half] = real.astype(jnp.bfloat16).reshape(per, half, feat)
-        second[span, half:] = imag.astype(jnp.bfloat16).reshape(per, half, feat)
+        second[span, :mode] = real.astype(jnp.bfloat16).reshape(each, mode, feat)
+        second[span, mode:] = imag.astype(jnp.bfloat16).reshape(each, mode, feat)
+
+        @pl.when(p < relayed)
+        def _():
+            ship(p).start()
+
         return 0
 
-    lax.fori_loop(0, held // per, mix, 0)
-
-    def wait_sent(r):
+    lax.fori_loop(0, packs, mix, 0)
+
+    def wait_sent(r, _):
         whole = sent.at[r, pl.ds(0, groups - 1)]
         pltpu.make_async_copy(whole, whole, fwd_send.at[r]).wait()
-
-    def lat_out(b):
-        def step(k, _):
-            both = dot(inverse[b], second[k]).astype(jnp.bfloat16)
-            turned[k] = both[: nb * groups]
-            turned[held + k] = both[nb * groups :]
+        return 0
+
+    lax.fori_loop(0, rows, wait_sent, 0)
+
+    pair = PACK // half
+    span_in = nb * groups
+    span_out = rows * half
+
+    def spread_rows(read, group, p, to_own, buffer, a, b, sem):
+        to = side_at if to_own else far_side
+
+        def lat(k, _):
+            both = dot(inverse[to], read(k)).astype(jnp.bfloat16)
+            for r in range(2):
+                for c, start in enumerate(range(0, span_out, span_in)):
+                    size = min(span_in, span_out - start)
+                    at = r * span_out + start
+                    turned[c * PACK + r * each + k, :size] = both[at : at + size]
             return 0
 
-        lax.fori_loop(0, held, step, 0, unroll=4)
-
-        def send_row(r, _):
-            j = b * nb + r
-            wait_sent(j)
-            place = pl.ds(pl.multiple_of(r * groups, PACK), groups)
-            for p in range(packs):
-                block = turned[p * PACK : (p + 1) * PACK, place, :].reshape(groups * PACK, feat)
-                moved = dot(turn_back[...], block).astype(jnp.bfloat16)
-                sent[j, :, p * PACK : (p + 1) * PACK, :] = moved.reshape(groups, PACK, feat)
-            other[j, spot, :] = sent[j, me]
-            for t in partners:
+        lax.fori_loop(0, each, lat, 0, unroll=4)
+        spot = pl.ds(pl.multiple_of(group * width + p * PACK, PACK), PACK)
+        cut = pl.ds(pl.multiple_of(b * PACK, PACK), PACK)
+
+        def send(i, _):
+            per = span_in // PACK
+            lead = pl.ds(i // per * PACK, PACK)
+            block = turned[lead, pl.ds(pl.multiple_of(lax.rem(i, per) * PACK, PACK), PACK), :]
+            moved = dot(turn[...], block.reshape(PACK * PACK, feat)).astype(jnp.bfloat16)
+            span = pl.ds(i * pair, pair)
+            buffer[span, pl.ds(a * half, half), cut, :] = moved.reshape(pair, half, PACK, feat)
+            if to_own:
+                other[span, spot, :] = buffer[span, a * half + place_at, cut, :]
+            for o in range(half - 1, 0 if to_own else -1, -1):
+                t = place_at ^ o
                 pltpu.make_async_remote_copy(
-                    src_ref=sent.at[j, t],
-                    dst_ref=other.at[j, spot],
-                    send_sem=back_send.at[j],
-                    recv_sem=back_recv.at[j],
-                    device_id={"grid": t},
+                    src_ref=buffer.at[span, a * half + t, cut],
+                    dst_ref=other.at[span, spot],
+                    send_sem=sem,
+                    recv_sem=back_recv.at[i],
+                    device_id={"grid": to * half + t},
                     device_id_type=MESH,
                 ).start()
             return 0
 
-        lax.fori_loop(0, nb, send_row, 0)
+        lax.fori_loop(0, rows // pair, send, 0)
+
+    def own_rows(p, _):
+        spread_rows(lambda k: second[p * each + k], me, p, True, sent, 0, p, back_send.at[p])
+        return 0
+
+    lax.fori_loop(0, packs, own_rows, 0)
+    last = packs - 1
+    spread_rows(lambda k: second[last * each + k], me, last, False, sent, 1, last, back_send.at[packs])
+
+    @pl.when(inner)
+    def _():
+        def relay_rows(q, _):
+            p, u = q // 2, lax.rem(q, 2)
+            group = (1 + far_side + u * (2 * far_side - 1)) * quarter + lane_at
+            got = far.at[u, pl.ds(p * each, each)]
+            pltpu.make_async_copy(got, got, far_recv.at[u * relayed + p]).wait()
+            sem = back_send.at[packs + 1 + q]
+            spread_rows(lambda k: far[u, p * each + k], group, p, True, arrived, u, p, sem)
+            return 0
+
+        lax.fori_loop(0, 2 * relayed, relay_rows, 0)
 
     def put(j, slot):
         return pltpu.make_async_copy(result.at[slot], out.at[j], out_sem.at[slot])
 
-    def finish(j):
-        whole = other.at[j, pl.ds(0, (groups - 1) * width)]
-        pltpu.make_async_copy(whole, whole, back_recv.at[j]).wait()
+    def finish(j, slot, more):
         weight = jnp.where(waves[...] == 0, 1.0, 2.0)
         weight = jnp.where(waves[...] < counts[j], weight, 0.0)
         spec = (other[j].astype(jnp.float32) * weight).astype(jnp.bfloat16)
         total = attended[j].astype(jnp.float32) + dot(back_table[...], spec)
-        slot = lax.rem(j, 2)
-
-        @pl.when(j >= 2)
-        def _():
-            put(j - 2, slot).wait()
+
+        @pl.when(more)
+        def _():
+            put(j, slot).wait()
 
         result[slot] = total.astype(jnp.bfloat16)
         put(j, slot).start()
 
     def phase_out(i, _):
-        @pl.when((i < rows) & (lax.rem(i, nb) == 0))
-        def _():
-            lat_out(i // nb)
-
-        @pl.when(i >= nb)
-        def _():
-            finish(i - nb)
-
+        span = pl.ds(i * pair, pair)
+
+        @pl.when(inner)
+        def _():
+            whole = other.at[span, pl.ds(0, (groups - 1) * width - 2 * relayed * PACK)]
+            pltpu.make_async_copy(whole, whole, back_recv.at[i]).wait()
+
+        @pl.when(jnp.logical_not(inner))
+        def _():
+            whole = other.at[span, pl.ds(0, (groups - 1) * width)]
+            pltpu.make_async_copy(whole, whole, back_recv.at[i]).wait()
+
+        for r in range(pair):
+            finish(i * pair + r, r, i > 0)
         return 0
 
-    lax.fori_loop(0, rows + nb, phase_out, 0)
+    lax.fori_loop(0, rows // pair, phase_out, 0)
 
     def drain(r, _):
         swap(r).wait_send()
-        whole = sent.at[r, pl.ds(0, groups - 1)]
-        pltpu.make_async_copy(whole, whole, back_send.at[r]).wait()
         return 0
 
     lax.fori_loop(0, rows, drain, 0)
-    for j in range(rows - 2, rows):
-        put(j, j % 2).wait()
+    for p in range(relayed):
+        ship(p).wait_send()
+    most = sent.at[:, pl.ds(0, half), pl.ds(0, PACK)]
+    fewer = sent.at[:, pl.ds(0, half - 1), pl.ds(0, PACK)]
+    for p in range(packs):
+        pltpu.make_async_copy(fewer, fewer, back_send.at[p]).wait()
+    pltpu.make_async_copy(most, most, back_send.at[packs]).wait()
+
+    @pl.when(inner)
+    def _():
+        for q in range(2 * relayed):
+            pltpu.make_async_copy(fewer, fewer, back_send.at[packs + 1 + q]).wait()
+
+    for r in range(pair):
+        put(rows - pair + r, r).wait()
 
 
 def fused(mesh_sizes, fields, mode_counts, gain_attn, w_query, w_key, w_value, w_out, gain_spec, w_first, w_second):
@@ -622,7 +708,7 @@
     waves = jnp.asarray(np_wave_order(groups)[1][:, None], dtype=jnp.int32)
     operands = [
         mode_counts, fields, gain_attn[None, :], w_query, w_key, w_value, w_out, gain_spec[None, :],
-        np_lon_forward(points, groups), heads, waves, forward, inverse, turn, turn.T, spread,
+        np_lon_forward(points, groups), heads, waves, forward, inverse, turn, spread,
         w_first.reshape(2, feat, block), w_second.reshape(2, feat, block),
     ]
     vmem = pl.BlockSpec(memory_space=pltpu.VMEM)
@@ -644,6 +730,7 @@
             pltpu.VMEM((width, nb * groups, feat), half),
             pltpu.VMEM((held, 2 * KLAT, feat), jnp.float32),
             pltpu.VMEM((held, 2 * KLAT, feat), half),
+            pltpu.VMEM((2, held - PACK // 2, 2 * KLAT, feat), half),
             pltpu.VMEM((points, feat), half),
             pltpu.VMEM((points, 2 * KLON), half),
             pltpu.VMEM((4, feat, feat), half),
@@ -653,8 +740,10 @@
             dma((rows,)),
             dma((rows,)),
             dma((rows,)),
-            dma((rows,)),
-            dma((rows,)),
+            dma((width // PACK - 1,)),
+            dma((2 * (width // PACK - 1),)),
+            dma((3 * (width // PACK),)),
+            dma((rows // 2,)),
             dma((2,)),
         ],
         compiler_params=pltpu.CompilerParams(
@@ -675,6 +764,7 @@
         and feat % 128 == 0
         and lat_dev % 2 == 0
         and width % PACK == 0
+        and width > PACK
     )
 
 

time: 447 us -> 416 us (0.931)
  Pallas kernels: 439 us -> 407 us
    pallas_call x1, Pallas kernels: 439 us -> 407 us  [fused(): pl.pallas_call(functools.partial(layer_kernel, points // 3 if points % 48...]
where the time goes in v1:
time: 416 us
  Pallas kernels  407 us (98%)
  local copies, waits for them, and re-layouts  8.33 us (2%)
    pallas_call x1, Pallas kernels, fused(): pl.pallas_call(functools.partial(layer_kernel, points // 3 if points % 48...  407 us
    unnamed x1, local copies, waits for them, and re-layouts  8.33 us

profile of v1, /device:TPU:0, one launch (start us, length us, event | category | flops | bytes accessed | tf_op | source)
XLA Modules:
  0.0 415.6 jit_solution(15031802851246649761)
XLA Ops:
  0.0 407.2 %layer.1 = bf16[24,768,256]{2,1,0:T(8,128)(2,1)} custom-call(s32[24]{0:T(128)} %counts.1, bf16[24,768,256]{2,1,0:T(8,128)(2,1)} %bitcast.7, f32[1,256]{1,0:T(1,128)} %bitcast.10, bf16[256,256]{1,0:T(8,128)(2,1)} %w_query.1, bf16[256,256]{1,0:T(8,128)(2,1)} %w_key.1, bf16[256,256]{1,0:T(8,128)(2,1)} %w_value.1, bf16[256,256]{1,0:T(8,128)(2,1)} %w_out.1, ...), custom_call_target="tpu_custom_call" | custom-call | tf_op jit(solution)/shard_map/layer/pallas_call | solution.py:719
  407.2 8.3 %copy.19 = bf16[1,24,768,256]{3,2,1,0:T(8,128)(2,1)} copy(bf16[1,24,768,256]{3,2,1,0:T(8,128)(2,1)} %bitcast.6) | data formatting | bytes 18874368

commit v2 on v1

--- a/solution.py
+++ b/solution.py
@@ -338,9 +338,22 @@
     return jnp.asarray(turn, dtype=jnp.bfloat16)
 
 
+def enter_kernel(points_sub, nb, held_count, counts, fields, *refs):
+    sources, out, held_refs = refs[:held_count], refs[held_count], refs[held_count + 1 : 2 * held_count + 1]
+    rest, sems = refs[2 * held_count + 1 : -1], refs[-1]
+    copies = [
+        pltpu.make_async_copy(source, target, sems.at[i])
+        for i, (source, target) in enumerate(zip(sources, held_refs))
+    ]
+    for copy in copies:
+        copy.start()
+    layer_kernel(points_sub, nb, copies, counts, fields, *held_refs, out, *rest)
+
+
 def layer_kernel(
     points_sub,
     nb,
+    copies,
     counts,
     fields,
     gain_one,
@@ -411,12 +424,15 @@
     pl.semaphore_signal(barrier, inc=1, device_id={"ens": 1 - member}, device_id_type=MESH)
     pl.semaphore_wait(barrier, groups)
 
-    def swap(r):
+    thirds = points // sub
+
+    def swap(r, s):
+        span = pl.ds(s * sub, sub)
         return pltpu.make_async_remote_copy(
-            src_ref=fields.at[r],
-            dst_ref=other.at[r],
+            src_ref=fields.at[r, span],
+            dst_ref=other.at[r, span],
             send_sem=swap_send.at[r],
-            recv_sem=swap_recv.at[r],
+            recv_sem=swap_recv.at[r * thirds + s],
             device_id={"ens": 1 - member},
             device_id_type=MESH,
         )
@@ -426,8 +442,11 @@
 
     ahead = min(SWAP_AHEAD, rows)
     for r in range(ahead):
-        swap(r).start()
+        for s in range(thirds):
+            swap(r, s).start()
     fetch(0, 0).start()
+    for copy in copies:
+        copy.wait()
 
     eye = lax.broadcasted_iota(jnp.int32, (feat, feat), 0) // HEAD
     same = eye == lax.broadcasted_iota(jnp.int32, (feat, feat), 1) // HEAD
@@ -446,14 +465,14 @@
         def _():
             fetch(r + 1, 1 - slot).start()
 
-        swap(r).wait_recv()
-
         @pl.when(r + ahead < rows)
         def _():
-            swap(r + ahead).start()
-
-        for start in range(0, points, sub):
-            span = pl.ds(start, sub)
+            for s in range(thirds):
+                swap(r + ahead, s).start()
+
+        for s in range(thirds):
+            swap(r, s).wait_recv()
+            span = pl.ds(s * sub, sub)
             field = own[slot, span, :].astype(jnp.float32)
             norm = layer_norm(field, gain_one[...])
             queries = dot(norm, w_query[...]).astype(jnp.bfloat16).astype(jnp.float32)
@@ -556,7 +575,7 @@
         second[span, :mode] = real.astype(jnp.bfloat16).reshape(each, mode, feat)
         second[span, mode:] = imag.astype(jnp.bfloat16).reshape(each, mode, feat)
 
-        @pl.when(p < relayed)
+        @pl.when(inner & (p < relayed))
         def _():
             ship(p).start()
 
@@ -619,6 +638,12 @@
         return 0
 
     lax.fori_loop(0, packs, own_rows, 0)
+
+    @pl.when(jnp.logical_not(inner))
+    def _():
+        for p in range(relayed):
+            ship(p).start()
+
     last = packs - 1
     spread_rows(lambda k: second[last * each + k], me, last, False, sent, 1, last, back_send.at[packs])
 
@@ -671,7 +696,7 @@
     lax.fori_loop(0, rows // pair, phase_out, 0)
 
     def drain(r, _):
-        swap(r).wait_send()
+        pltpu.make_async_copy(fields.at[r], fields.at[r], swap_send.at[r]).wait()
         return 0
 
     lax.fori_loop(0, rows, drain, 0)
@@ -711,17 +736,19 @@
         np_lon_forward(points, groups), heads, waves, forward, inverse, turn, spread,
         w_first.reshape(2, feat, block), w_second.reshape(2, feat, block),
     ]
-    vmem = pl.BlockSpec(memory_space=pltpu.VMEM)
     hbm = pl.BlockSpec(memory_space=pl.ANY)
-    specs = [pl.BlockSpec(memory_space=pltpu.SMEM), hbm] + [vmem] * (len(operands) - 2)
+    specs = [pl.BlockSpec(memory_space=pltpu.SMEM)] + [hbm] * (len(operands) - 1)
+    held_operands = operands[2:]
+    sub = points // 3 if points % 48 == 0 else points
     half = jnp.bfloat16
     dma = pltpu.SemaphoreType.DMA
     out = pl.pallas_call(
-        functools.partial(layer_kernel, points // 3 if points % 48 == 0 else points, nb),
+        functools.partial(enter_kernel, sub, nb, len(held_operands)),
         in_specs=specs,
         out_specs=hbm,
         out_shape=jax.ShapeDtypeStruct((rows, points, feat), half),
-        scratch_shapes=[
+        scratch_shapes=[pltpu.VMEM(o.shape, o.dtype) for o in held_operands]
+        + [
             pltpu.VMEM((2, points, feat), half),
             pltpu.VMEM((rows, points, feat), half),
             pltpu.VMEM((rows, points, feat), half),
@@ -737,7 +764,7 @@
             pltpu.VMEM((2, points, feat), half),
             dma((2,)),
             dma((rows,)),
-            dma((rows,)),
+            dma((rows * (points // sub),)),
             dma((rows,)),
             dma((rows,)),
             dma((width // PACK - 1,)),
@@ -745,6 +772,7 @@
             dma((3 * (width // PACK),)),
             dma((rows // 2,)),
             dma((2,)),
+            dma((len(held_operands),)),
         ],
         compiler_params=pltpu.CompilerParams(
             collective_id=0, has_side_effects=True, vmem_limit_bytes=67043328

time: 416 us -> 400 us (0.962)
  Pallas kernels: 407 us -> 391 us
    pallas_call x1, Pallas kernels: 407 us -> 391 us  [fused(): pl.pallas_call(functools.partial(enter_kernel, sub, nb, len(held_operands...]
where the time goes in v2:
time: 400 us
  Pallas kernels  391 us (98%)
  local copies, waits for them, and re-layouts  8.33 us (2%)
    pallas_call x1, Pallas kernels, fused(): pl.pallas_call(functools.partial(enter_kernel, sub, nb, len(held_operands...  391 us
    unnamed x1, local copies, waits for them, and re-layouts  8.33 us

profile of v2, /device:TPU:0, one launch (start us, length us, event | category | flops | bytes accessed | tf_op | source)
XLA Modules:
  0.0 399.6 jit_solution(15215397186251786693)
XLA Ops:
  0.0 391.3 %layer.1 = bf16[24,768,256]{2,1,0:T(8,128)(2,1)} custom-call(s32[24]{0:T(128)} %counts.1, bf16[24,768,256]{2,1,0:T(8,128)(2,1)} %bitcast.7, f32[1,256]{1,0:T(1,128)} %bitcast.10, bf16[256,256]{1,0:T(8,128)(2,1)} %refs_1_.1, bf16[256,256]{1,0:T(8,128)(2,1)} %refs_2_.1, bf16[256,256]{1,0:T(8,128)(2,1)} %refs_3_.1, bf16[256,256]{1,0:T(8,128)(2,1)} %refs_4_.1, ...), custom_call_target="tpu_custom_call" | custom-call | tf_op jit(solution)/shard_map/layer/pallas_call | solution.py:745
  391.3 8.3 %copy.19 = bf16[1,24,768,256]{3,2,1,0:T(8,128)(2,1)} copy(bf16[1,24,768,256]{3,2,1,0:T(8,128)(2,1)} %bitcast.6) | data formatting | bytes 18874368

commit v3 on v2

--- a/solution.py
+++ b/solution.py
@@ -371,10 +371,9 @@
     spread,
     w_first,
     w_second,
-    out,
+    attended,
     own,
     other,
-    attended,
     sent,
     arrived,
     turned,
@@ -384,7 +383,6 @@
     normed,
     back_table,
     blocks,
-    result,
     own_sem,
     swap_send,
     swap_recv,
@@ -394,7 +392,6 @@
     far_recv,
     back_send,
     back_recv,
-    out_sem,
 ):
     rows, groups, width, feat = sent.shape
     points = other.shape[1]
@@ -650,7 +647,7 @@
     @pl.when(inner)
     def _():
         def relay_rows(q, _):
-            p, u = q // 2, lax.rem(q, 2)
+            u, p = q // relayed, lax.rem(q, relayed)
             group = (1 + far_side + u * (2 * far_side - 1)) * quarter + lane_at
             got = far.at[u, pl.ds(p * each, each)]
             pltpu.make_async_copy(got, got, far_recv.at[u * relayed + p]).wait()
@@ -660,21 +657,12 @@
 
         lax.fori_loop(0, 2 * relayed, relay_rows, 0)
 
-    def put(j, slot):
-        return pltpu.make_async_copy(result.at[slot], out.at[j], out_sem.at[slot])
-
-    def finish(j, slot, more):
+    def finish(j):
         weight = jnp.where(waves[...] == 0, 1.0, 2.0)
         weight = jnp.where(waves[...] < counts[j], weight, 0.0)
         spec = (other[j].astype(jnp.float32) * weight).astype(jnp.bfloat16)
         total = attended[j].astype(jnp.float32) + dot(back_table[...], spec)
-
-        @pl.when(more)
-        def _():
-            put(j, slot).wait()
-
-        result[slot] = total.astype(jnp.bfloat16)
-        put(j, slot).start()
+        attended[j] = total.astype(jnp.bfloat16)
 
     def phase_out(i, _):
         span = pl.ds(i * pair, pair)
@@ -690,7 +678,7 @@
             pltpu.make_async_copy(whole, whole, back_recv.at[i]).wait()
 
         for r in range(pair):
-            finish(i * pair + r, r, i > 0)
+            finish(i * pair + r)
         return 0
 
     lax.fori_loop(0, rows // pair, phase_out, 0)
@@ -712,9 +700,6 @@
     def _():
         for q in range(2 * relayed):
             pltpu.make_async_copy(fewer, fewer, back_send.at[packs + 1 + q]).wait()
-
-    for r in range(pair):
-        put(rows - pair + r, r).wait()
 
 
 def fused(mesh_sizes, fields, mode_counts, gain_attn, w_query, w_key, w_value, w_out, gain_spec, w_first, w_second):
@@ -745,12 +730,11 @@
     out = pl.pallas_call(
         functools.partial(enter_kernel, sub, nb, len(held_operands)),
         in_specs=specs,
-        out_specs=hbm,
-        out_shape=jax.ShapeDtypeStruct((rows, points, feat), half),
+        out_specs=pl.BlockSpec(memory_space=pltpu.VMEM),
+        out_shape=pltpu.VMEM((rows, points, feat), half),
         scratch_shapes=[pltpu.VMEM(o.shape, o.dtype) for o in held_operands]
         + [
             pltpu.VMEM((2, points, feat), half),
-            pltpu.VMEM((rows, points, feat), half),
             pltpu.VMEM((rows, points, feat), half),
             pltpu.VMEM((rows, groups, width, feat), half),
             pltpu.VMEM((rows, groups, width, feat), half),
@@ -761,7 +745,6 @@
             pltpu.VMEM((points, feat), half),
             pltpu.VMEM((points, 2 * KLON), half),
             pltpu.VMEM((4, feat, feat), half),
-            pltpu.VMEM((2, points, feat), half),
             dma((2,)),
             dma((rows,)),
             dma((rows * (points // sub),)),
@@ -771,11 +754,10 @@
             dma((2 * (width // PACK - 1),)),
             dma((3 * (width // PACK),)),
             dma((rows // 2,)),
-            dma((2,)),
             dma((len(held_operands),)),
         ],
         compiler_params=pltpu.CompilerParams(
-            collective_id=0, has_side_effects=True, vmem_limit_bytes=67043328
+            collective_id=0, has_side_effects=True, vmem_limit_bytes=67043328 - rows * points * feat * 2
         ),
         name="layer",
     )(*operands)

time: 400 us -> 389 us (0.973)
  Pallas kernels: 391 us -> 386 us
  local copies, waits for them, and re-layouts: 8.33 us -> 3.74 us
    pallas_call x1, Pallas kernels: 391 us -> 386 us  [fused(): pl.pallas_call(functools.partial(enter_kernel, sub, nb, len(held_operands...]
    unnamed x1, local copies, waits for them, and re-layouts: 8.33 us -> 3.74 us
where the time goes in v3:
time: 389 us
  Pallas kernels  386 us (99%)
    pallas_call x1, Pallas kernels, fused(): pl.pallas_call(functools.partial(enter_kernel, sub, nb, len(held_operands...  386 us

profile of v3, /device:TPU:0, one launch (start us, length us, event | category | flops | bytes accessed | tf_op | source)
XLA Modules:
  0.0 389.3 jit_solution(12772038569179349219)
XLA Ops:
  0.0 385.5 %layer.1 = bf16[24,768,256]{2,1,0:T(8,128)(2,1)S(1)} custom-call(s32[24]{0:T(128)} %counts.1, bf16[24,768,256]{2,1,0:T(8,128)(2,1)} %bitcast.7, f32[1,256]{1,0:T(1,128)} %bitcast.10, bf16[256,256]{1,0:T(8,128)(2,1)} %refs_1_.1, bf16[256,256]{1,0:T(8,128)(2,1)} %refs_2_.1, bf16[256,256]{1,0:T(8,128)(2,1)} %refs_3_.1, bf16[256,256]{1,0:T(8,128)(2,1)} %refs_4_.1, ...), custom_call_target="tpu_custom_call" | custom-call | tf_op jit(solution)/shard_map/layer/pallas_call | solution.py:730
  385.5 3.7 copy.19

commit v4 on v3

--- a/solution.py
+++ b/solution.py
@@ -392,6 +392,7 @@
     far_recv,
     back_send,
     back_recv,
+    go_sem,
 ):
     rows, groups, width, feat = sent.shape
     points = other.shape[1]
@@ -412,6 +413,7 @@
     lane_at = lax.rem(me, quarter)
     inner = me // quarter == 1 + side_at
     relay = (1 + far_side) * quarter + lane_at
+    outer = 3 * side_at * quarter + lane_at
     slot_at = jnp.where(inner, 0, 1)
     relayed = packs - 1
 
@@ -553,9 +555,9 @@
         span = pl.ds(p * each, each)
         return pltpu.make_async_remote_copy(
             src_ref=second.at[span],
-            dst_ref=far.at[slot_at, span],
+            dst_ref=far.at[pl.ds(slot_at * held + p * each, each)],
             send_sem=far_send.at[p],
-            recv_sem=far_recv.at[slot_at * relayed + p],
+            recv_sem=far_recv.at[slot_at * packs + p],
             device_id={"grid": relay},
             device_id_type=MESH,
         )
@@ -572,7 +574,7 @@
         second[span, :mode] = real.astype(jnp.bfloat16).reshape(each, mode, feat)
         second[span, mode:] = imag.astype(jnp.bfloat16).reshape(each, mode, feat)
 
-        @pl.when(inner & (p < relayed))
+        @pl.when(inner)
         def _():
             ship(p).start()
 
@@ -638,24 +640,32 @@
 
     @pl.when(jnp.logical_not(inner))
     def _():
+        pl.semaphore_wait(go_sem, 1)
         for p in range(relayed):
             ship(p).start()
-
-    last = packs - 1
-    spread_rows(lambda k: second[last * each + k], me, last, False, sent, 1, last, back_send.at[packs])
+        last = packs - 1
+        spread_rows(lambda k: second[last * each + k], me, last, False, sent, 1, last, back_send.at[packs])
 
     @pl.when(inner)
     def _():
         def relay_rows(q, _):
-            u, p = q // relayed, lax.rem(q, relayed)
+            u, p = q // packs, lax.rem(q, packs)
             group = (1 + far_side + u * (2 * far_side - 1)) * quarter + lane_at
-            got = far.at[u, pl.ds(p * each, each)]
-            pltpu.make_async_copy(got, got, far_recv.at[u * relayed + p]).wait()
+            base = u * held + p * each
+            got = far.at[pl.ds(base, each)]
+            pltpu.make_async_copy(got, got, far_recv.at[q]).wait()
+
+            @pl.when(q == packs - 1)
+            def _():
+                for each_pack in range(packs):
+                    ship(each_pack).wait_send()
+                pl.semaphore_signal(go_sem, inc=1, device_id={"grid": outer}, device_id_type=MESH)
+
             sem = back_send.at[packs + 1 + q]
-            spread_rows(lambda k: far[u, p * each + k], group, p, True, arrived, u, p, sem)
+            spread_rows(lambda k: far[base + k], group, p, True, arrived, u, p, sem)
             return 0
 
-        lax.fori_loop(0, 2 * relayed, relay_rows, 0)
+        lax.fori_loop(0, packs + relayed, relay_rows, 0)
 
     def finish(j):
         weight = jnp.where(waves[...] == 0, 1.0, 2.0)
@@ -669,7 +679,7 @@
 
         @pl.when(inner)
         def _():
-            whole = other.at[span, pl.ds(0, (groups - 1) * width - 2 * relayed * PACK)]
+            whole = other.at[span, pl.ds(0, (groups - 1) * width - (packs + relayed) * PACK)]
             pltpu.make_async_copy(whole, whole, back_recv.at[i]).wait()
 
         @pl.when(jnp.logical_not(inner))
@@ -688,18 +698,21 @@
         return 0
 
     lax.fori_loop(0, rows, drain, 0)
-    for p in range(relayed):
-        ship(p).wait_send()
     most = sent.at[:, pl.ds(0, half), pl.ds(0, PACK)]
     fewer = sent.at[:, pl.ds(0, half - 1), pl.ds(0, PACK)]
     for p in range(packs):
         pltpu.make_async_copy(fewer, fewer, back_send.at[p]).wait()
-    pltpu.make_async_copy(most, most, back_send.at[packs]).wait()
 
     @pl.when(inner)
     def _():
-        for q in range(2 * relayed):
+        for q in range(packs + relayed):
             pltpu.make_async_copy(fewer, fewer, back_send.at[packs + 1 + q]).wait()
+
+    @pl.when(jnp.logical_not(inner))
+    def _():
+        for p in range(relayed):
+            ship(p).wait_send()
+        pltpu.make_async_copy(most, most, back_send.at[packs]).wait()
 
 
 def fused(mesh_sizes, fields, mode_counts, gain_attn, w_query, w_key, w_value, w_out, gain_spec, w_first, w_second):
@@ -741,7 +754,7 @@
             pltpu.VMEM((width, nb * groups, feat), half),
             pltpu.VMEM((held, 2 * KLAT, feat), jnp.float32),
             pltpu.VMEM((held, 2 * KLAT, feat), half),
-            pltpu.VMEM((2, held - PACK // 2, 2 * KLAT, feat), half),
+            pltpu.VMEM((2 * held - PACK // 2, 2 * KLAT, feat), half),
             pltpu.VMEM((points, feat), half),
             pltpu.VMEM((points, 2 * KLON), half),
             pltpu.VMEM((4, feat, feat), half),
@@ -750,10 +763,11 @@
             dma((rows * (points // sub),)),
             dma((rows,)),
             dma((rows,)),
-            dma((width // PACK - 1,)),
-            dma((2 * (width // PACK - 1),)),
+            dma((width // PACK,)),
+            dma((2 * (width // PACK) - 1,)),
             dma((3 * (width // PACK),)),
             dma((rows // 2,)),
+            pltpu.SemaphoreType.REGULAR,
             dma((len(held_operands),)),
         ],
         compiler_params=pltpu.CompilerParams(

time: 389 us -> 388 us (level)
  no operation moved by 1% of the time
where the time goes in v4:
time: 388 us
  Pallas kernels  384 us (99%)
    pallas_call x1, Pallas kernels, fused(): pl.pallas_call(functools.partial(enter_kernel, sub, nb, len(held_operands...  384 us

profile of v4, /device:TPU:0, one launch (start us, length us, event | category | flops | bytes accessed | tf_op | source)
XLA Modules:
  0.0 387.7 jit_solution(9822963806938218103)
XLA Ops:
  0.0 383.9 %layer.1 = bf16[24,768,256]{2,1,0:T(8,128)(2,1)S(1)} custom-call(s32[24]{0:T(128)} %counts.1, bf16[24,768,256]{2,1,0:T(8,128)(2,1)} %bitcast.7, f32[1,256]{1,0:T(1,128)} %bitcast.10, bf16[256,256]{1,0:T(8,128)(2,1)} %refs_1_.1, bf16[256,256]{1,0:T(8,128)(2,1)} %refs_2_.1, bf16[256,256]{1,0:T(8,128)(2,1)} %refs_3_.1, bf16[256,256]{1,0:T(8,128)(2,1)} %refs_4_.1, ...), custom_call_target="tpu_custom_call" | custom-call | tf_op jit(solution)/shard_map/layer/pallas_call | solution.py:743
  383.9 3.7 copy.19

commit v5 on v4

--- a/solution.py
+++ b/solution.py
@@ -524,7 +524,7 @@
             rows_spec[k] += dot(forward[b], pair)
             return 0
 
-        lax.fori_loop(0, count, step, 0, unroll=4)
+        lax.fori_loop(0, count, step, 0, unroll=8)
 
     def phase_in(i, _):
         @pl.when(i < rows)
@@ -605,7 +605,7 @@
                     turned[c * PACK + r * each + k, :size] = both[at : at + size]
             return 0
 
-        lax.fori_loop(0, each, lat, 0, unroll=4)
+        lax.fori_loop(0, each, lat, 0, unroll=8)
         spot = pl.ds(pl.multiple_of(group * width + p * PACK, PACK), PACK)
         cut = pl.ds(pl.multiple_of(b * PACK, PACK), PACK)
 
@@ -630,7 +630,7 @@
                 ).start()
             return 0
 
-        lax.fori_loop(0, rows // pair, send, 0)
+        lax.fori_loop(0, rows // pair, send, 0, unroll=2)
 
     def own_rows(p, _):
         spread_rows(lambda k: second[p * each + k], me, p, True, sent, 0, p, back_send.at[p])

time: 388 us -> 387 us (level)
  no operation moved by 1% of the time
where the time goes in v5:
time: 387 us
  Pallas kernels  383 us (99%)
    pallas_call x1, Pallas kernels, fused(): pl.pallas_call(functools.partial(enter_kernel, sub, nb, len(held_operands...  383 us

profile of v5, /device:TPU:0, one launch (start us, length us, event | category | flops | bytes accessed | tf_op | source)
XLA Modules:
  0.0 386.6 jit_solution(4134228224640903936)
XLA Ops:
  0.0 382.9 %layer.1 = bf16[24,768,256]{2,1,0:T(8,128)(2,1)S(1)} custom-call(s32[24]{0:T(128)} %counts.1, bf16[24,768,256]{2,1,0:T(8,128)(2,1)} %bitcast.7, f32[1,256]{1,0:T(1,128)} %bitcast.10, bf16[256,256]{1,0:T(8,128)(2,1)} %refs_1_.1, bf16[256,256]{1,0:T(8,128)(2,1)} %refs_2_.1, bf16[256,256]{1,0:T(8,128)(2,1)} %refs_3_.1, bf16[256,256]{1,0:T(8,128)(2,1)} %refs_4_.1, ...), custom_call_target="tpu_custom_call" | custom-call | tf_op jit(solution)/shard_map/layer/pallas_call | solution.py:743
  382.9 3.7 copy.19
